TPU v7x, 32 devices: a whole 2x2x4 slice. The times are simulated.
32 devices in a mesh: tile: 8 (over y, x, core), mode: 4 (over z).
Axes of the slice: x: 2, y: 2, z: 4, core: 2. Of those that a mesh axis runs over, the one named last changes fastest.
Arguments:
- object_field: float32 [2, 2, 2048, 384], P(None, None, 'tile'), may hold values from -4 to 4
- probe: float32 [8, 2, 256, 256], P('mode'), may hold values from -4 to 4
- measured: float32 [32, 256, 256], P('tile'), may hold values from 0 to 16
- prop_phase: float32 [256, 256], replicated, may hold values from -3.140625 to 3.140625
- counts: int32 [8], P('tile'), may hold values from 1 to 4, 16 in all
- row_offset: int32 [32], P('tile'), may hold values from 0 to 255
- col_offset: int32 [32], P('tile'), may hold values from 0 to 128
Outputs:
- object_grad: float32 [2, 2, 2048, 384], P(None, None, 'tile')
- probe_grad: float32 [8, 2, 256, 256], P('mode')
Inputs may be any that keep to these rules, and one draw needn't show every extreme that they name: Slot i is live for i % 4 < counts[i // 4]; some tile has all 4 slots live.
All inputs are finite; a program needn't handle non-finite values. No bound on the sum of `counts` on one device may be relied on, other than what follows from the above.
Results may differ from a plain program's by a relative error of at most 0.0003.
Values sent between devices are 32-bit elements; how exact they have to be, the bound alone decides.
A program may use at most 128 MiB of HBM per device.

v0:
```python
import math

import jax
import jax.numpy as jnp
from jax import lax
from jax.sharding import PartitionSpec as P

MODES = 8


HIGH = lax.Precision.HIGHEST


def shifted(block, axis, distance):
    devices = range(lax.axis_size(axis))
    route = [(i - distance, i) for i in devices if i - distance in devices]
    return lax.ppermute(block, axis, route)


def dft_tables(length):
    indices = jnp.arange(length, dtype=jnp.int32)
    product = indices[:, None] * indices[None, :] % length
    angle = product.astype(jnp.float32) * (2.0 * math.pi / length)
    factor = 1.0 / math.sqrt(length)
    return (jnp.cos(angle) * factor, jnp.sin(angle) * factor)


def on_left(matrix, field):
    return jnp.einsum("jk,mkl->mjl", matrix, field, precision=HIGH)


def on_right(field, matrix):
    return jnp.einsum("mjk,kl->mjl", field, matrix, precision=HIGH)


def transform(pair, tables, sign):
    cosine, sine = tables
    real_in, imag_in = pair
    mid_real = on_left(cosine, real_in) - sign * on_left(sine, imag_in)
    mid_imag = on_left(cosine, imag_in) + sign * on_left(sine, real_in)
    out_real = on_right(mid_real, cosine) - sign * on_right(mid_imag, sine)
    out_imag = on_right(mid_imag, cosine) + sign * on_right(mid_real, sine)
    return (out_real, out_imag)


def times(first, second):
    return (
        first[0] * second[0] - first[1] * second[1],
        first[0] * second[1] + first[1] * second[0],
    )


def times_conj(first, second):
    return (
        first[0] * second[0] + first[1] * second[1],
        first[0] * second[1] - first[1] * second[0],
    )


def forward_pass(window, probe_pair, kernel, tables):
    wave = times(probe_pair, (window[0, 0], window[0, 1]))
    spectrum = transform(wave, tables, -1.0)
    moved = transform(times(kernel, spectrum), tables, 1.0)
    before = [moved]
    wave = times(moved, (window[1, 0], window[1, 1]))
    far_field = transform(wave, tables, -1.0)
    return (before, far_field)


def backward_pass(window, before, far_field, weight, probe_pair, kernel, tables):
    layers = window.shape[0]
    back = transform((weight * far_field[0], weight * far_field[1]), tables, 1.0)
    pieces = [None] * layers
    term = times_conj(before[0], back)
    pieces[1] = jnp.stack([jnp.sum(term[0], axis=0), jnp.sum(term[1], axis=0)])
    inner = transform(times_conj((window[1, 0], window[1, 1]), back), tables, -1.0)
    back = transform(times_conj(kernel, inner), tables, 1.0)
    first = times_conj(probe_pair, back)
    pieces[0] = jnp.stack([jnp.sum(first[0], axis=0), jnp.sum(first[1], axis=0)])
    probe_term = times_conj((window[0, 0], window[0, 1]), back)
    return (jnp.stack(pieces), jnp.stack([probe_term[0], probe_term[1]], axis=1))


def per_device(object_field, probe, measured, prop_phase, counts, row_offset, col_offset):
    layers, _, tile_rows, columns = object_field.shape
    width = probe.shape[-1]
    next_rows = shifted(object_field, "tile", -1)
    extended = jnp.concatenate([object_field, next_rows], axis=2)
    tables = dft_tables(width)
    kernel = (jnp.cos(prop_phase), jnp.sin(prop_phase))
    probe_pair = (probe[:, 0], probe[:, 1])
    live_count = counts[0]
    zero_index = jnp.zeros((), jnp.int32)
    slot_total = row_offset.shape[0]

    def cut_window(row_start, col_start):
        start = (zero_index, zero_index, row_start, col_start)
        return lax.dynamic_slice(extended, start, (layers, 2, width, width))

    def place_terms(grad_ext, pieces, row_start, col_start):
        start = (zero_index, zero_index, row_start, col_start)
        current = lax.dynamic_slice(grad_ext, start, (layers, 2, width, width))
        return lax.dynamic_update_slice(grad_ext, current + pieces, start)

    init = (jnp.zeros(extended.shape, jnp.float32), jnp.zeros(probe.shape, jnp.float32))
    windows = jax.vmap(cut_window)(row_offset, col_offset)
    before, far_field = jax.vmap(lambda item: forward_pass(item, probe_pair, kernel, tables))(
        windows
    )
    local_power = jnp.sum(far_field[0] * far_field[0] + far_field[1] * far_field[1], axis=1)
    power = lax.psum(local_power, "mode")
    alive = (jnp.arange(slot_total, dtype=jnp.int32) < live_count).astype(jnp.float32)
    weight = (power - measured) / MODES * alive[:, None, None]

    def one_back(item, item_before, item_far, item_weight):
        return backward_pass(item, item_before, item_far, item_weight, probe_pair, kernel, tables)

    all_pieces, probe_terms = jax.vmap(one_back)(windows, before, far_field, weight)
    grad_probe = jnp.sum(probe_terms, axis=0)

    def add_slot(slot, grad_ext):
        return place_terms(grad_ext, all_pieces[slot], row_offset[slot], col_offset[slot])

    grad_ext = lax.fori_loop(zero_index, jnp.full((), slot_total, jnp.int32), add_slot, init[0])
    summed = lax.psum(grad_ext, "mode")
    arrived = shifted(summed[:, :, tile_rows:, :], "tile", 1)
    object_grad = summed[:, :, :tile_rows, :].at[:, :, :width, :].add(arrived)
    probe_grad = lax.psum(grad_probe, "tile")
    return (object_grad, probe_grad)


def solution(mesh):
    placed = (
        P(None, None, "tile", None),
        P("mode", None, None, None),
        P("tile", None, None),
        P(),
        P("tile"),
        P("tile"),
        P("tile"),
    )
    return jax.shard_map(
        per_device,
        mesh=mesh,
        in_specs=placed,
        out_specs=(P(None, None, "tile", None), P("mode", None, None, None)),
        check_vma=False,
    )
```

profile of v0, /device:TPU:0, one launch (start us, length us, event | category | flops | bytes accessed | tf_op | source)
XLA Modules:
  0.0 612.0 jit_solution(3632968894506634922)
XLA Ops:
  16.6 12.5 %while.14 = (s32[]{:T(128)}, f32[2,2,512,384]{3,2,1,0:T(8,128)S(1)}, s32[4,4]{1,0:T(4,128)S(1)}, f32[4,2,2,256,256]{4,3,2,1,0:T(8,128)}, s32[]{:T(128)}) while((s32[]{:T(128)}, f32[2,2,512,384]{3,2,1,0:T(8,128)S(1)}, s32[4,4]{1,0:T(4,128)S(1)}, f32[4,2,2,256,256]{4,3,2,1,0:T(8,128)}, s32[]{:T(128)}) %tuple.57), condition=%wide.while_cond.1, body=%wide.while_body.1.sunk | while | flops 2 | bytes 2098801 | solution.py:98
  40.8 4.7 multiply_add_fusion.9
  54.2 4.6 multiply_subtract_fusion.9
  63.4 4.6 multiply_subtract_fusion.8
  72.6 4.6 fusion.117
  77.2 5.0 convolution_add_fusion.1
  91.2 4.8 convolution_subtract_fusion.1
  104.9 4.8 fusion.165
  109.8 4.6 fusion.162
  114.4 5.0 multiply_add_fusion.5
  128.4 4.8 multiply_subtract_fusion.5
  137.7 7.2 %add_reduce_fusion.2 = (f32[4,256,256]{2,1,0:T(8,128)}, f32[4,2,256,256]{3,2,1,0:T(8,128)}) fusion(f32[4,2,256,256]{3,2,1,0:T(8,128)S(1)} %multiply_subtract_fusion.4, f32[4,2,256,256]{3,2,1,0:T(8,128)S(1)} %fusion.24, f32[4,2,256,256]{3,2,1,0:T(8,128)S(1)} %multiply_subtract_fusion.5), kind=kOutput, calls=%fused_computation.70 | convolution fusion | flops 1614479360 | bytes 9437184 | tf_op jit(solution)/shard_map/vmap(mjk,kl->mjl)/dot_general | solution.py:33
  145.8 67.6 %all-reduce.4.cloned.1.call-done = f32[4,256,256]{2,1,0:T(8,128)} async-done(((f32[4,256,256]{2,1,0:T(8,128)}), f32[4,256,256]{2,1,0:T(8,128)}) %all-reduce.4.cloned.1.call-update) | async-done | bytes 1048592 | tf_op jit(solution)/shard_map/psum | solution.py:111
  224.6 4.9 fusion.63
  238.7 4.7 fusion.60
  247.9 5.4 add_reduce_fusion
  253.3 4.6 fusion.155
  258.0 4.6 fusion.152
  262.6 5.1 multiply_add_fusion.2
  276.7 4.9 multiply_subtract_fusion.2
  290.7 4.8 fusion.118
  295.5 4.6 fusion.119
  300.1 5.0 convolution_add_fusion
  314.2 4.8 convolution_subtract_fusion
  323.5 7.5 %add_bitcast_fusion = (f32[4,2,1,256,256]{4,3,1,0,2:T(8,128)S(1)}, f32[4,2,1,256,256]{4,3,1,0,2:T(8,128)}, f32[4,256,256]{2,1,0:T(8,128)S(1)}, f32[4,256,256]{2,1,0:T(8,128)S(1)}) fusion(f32[4,2,256,256]{3,2,1,0:T(8,128)S(1)} %fusion.90, f32[4,256,256]{2,1,0:T(8,128)S(1)} %get-tuple-element.89, f32[4,256,256]{2,1,0:T(8,128)S(1)} %copy-done.5, ...), kind=kOutput, calls=%fused_computation.57 | convolution fusion | flops 1618935808 | bytes 15728640 | tf_op jit(solution)/shard_map/vmap(mjk,kl->mjl)/dot_general | solution.py:33
  335.6 75.8 %while.13 = (s32[]{:T(128)}, f32[2,2,512,384]{3,2,1,0:T(8,128)}, s32[4]{0:T(128)S(1)}, s32[4]{0:T(128)S(1)}, f32[4,2,2,256,256]{4,3,2,1,0:T(8,128)}, /*index=5*/s32[]{:T(128)}, s32[]{:T(128)}, s32[]{:T(128)}, s32[]{:T(128)}) while((s32[]{:T(128)}, f32[2,2,512,384]{3,2,1,0:T(8,128)}, s32[4]{0:T(128)S(1)}, s32[4]{0:T(128)S(1)}, ...), condition=%wide.region_7.8_spmd, body=%wide.region_6.7_spmd.sunk | while | flops 262152 | bytes 5243081 | solution.py:124
  342.7 11.9 %dynamic_update_slice.4 = f32[2,2,512,384]{3,2,1,0:T(8,128)} dynamic-update-slice(f32[2,2,512,384]{3,2,1,0:T(8,128)} %get-tuple-element.186, f32[2,2,256,256]{3,2,1,0:T(8,128)S(1)} %bitcast_add_fusion.2, s32[]{:T(128)} %constant.72.clone.1..sunk, s32[]{:T(128)} %constant.72.clone.1..sunk, s32[]{:T(128)S(6)} %select_n.288, s32[]{:T(128)S(6)} %select_n.289) | dynamic-update-slice | bytes 2097156 | tf_op jit(solution)/shard_map/while/body/dynamic_update_slice | solution.py:103
  361.8 11.6 %dynamic_update_slice.4 = f32[2,2,512,384]{3,2,1,0:T(8,128)} dynamic-update-slice(f32[2,2,512,384]{3,2,1,0:T(8,128)} %get-tuple-element.186, f32[2,2,256,256]{3,2,1,0:T(8,128)S(1)} %bitcast_add_fusion.2, s32[]{:T(128)} %constant.72.clone.1..sunk, s32[]{:T(128)} %constant.72.clone.1..sunk, s32[]{:T(128)S(6)} %select_n.288, s32[]{:T(128)S(6)} %select_n.289) | dynamic-update-slice | bytes 2097156 | tf_op jit(solution)/shard_map/while/body/dynamic_update_slice | solution.py:103
  380.6 11.8 %dynamic_update_slice.4 = f32[2,2,512,384]{3,2,1,0:T(8,128)} dynamic-update-slice(f32[2,2,512,384]{3,2,1,0:T(8,128)} %get-tuple-element.186, f32[2,2,256,256]{3,2,1,0:T(8,128)S(1)} %bitcast_add_fusion.2, s32[]{:T(128)} %constant.72.clone.1..sunk, s32[]{:T(128)} %constant.72.clone.1..sunk, s32[]{:T(128)S(6)} %select_n.288, s32[]{:T(128)S(6)} %select_n.289) | dynamic-update-slice | bytes 2097156 | tf_op jit(solution)/shard_map/while/body/dynamic_update_slice | solution.py:103
  399.6 11.8 %dynamic_update_slice.4 = f32[2,2,512,384]{3,2,1,0:T(8,128)} dynamic-update-slice(f32[2,2,512,384]{3,2,1,0:T(8,128)} %get-tuple-element.186, f32[2,2,256,256]{3,2,1,0:T(8,128)S(1)} %bitcast_add_fusion.2, s32[]{:T(128)} %constant.72.clone.1..sunk, s32[]{:T(128)} %constant.72.clone.1..sunk, s32[]{:T(128)S(6)} %select_n.288, s32[]{:T(128)S(6)} %select_n.289) | dynamic-update-slice | bytes 2097156 | tf_op jit(solution)/shard_map/while/body/dynamic_update_slice | solution.py:103
  411.5 119.6 %all-reduce.6.cloned.1.call-done = f32[2,2,512,384]{3,2,1,0:T(8,128)} async-done(((f32[2,2,512,384]{3,2,1,0:T(8,128)}), f32[2,2,512,384]{3,2,1,0:T(8,128)}) %all-reduce.6.cloned.1.call-update) | async-done | bytes 3145744 | tf_op jit(solution)/shard_map/psum | solution.py:125
  537.9 62.4 %all-reduce.8.cloned.1.call-done = f32[2,2,256,256]{3,2,0,1:T(8,128)} async-done(((f32[2,2,256,256]{3,2,0,1:T(8,128)}), f32[2,2,256,256]{3,2,0,1:T(8,128)}) %all-reduce.8.cloned.1.call-update) | async-done | bytes 1048592 | tf_op jit(solution)/shard_map/psum | solution.py:128
  (120 shorter events, 168.6 us)
Async XLA Ops:
  7.2 206.2 %all-reduce.4.cloned.1.call-start = ((), (), s32[]{:S(2)}) async-start(), calls=%async_computation | async-start | bytes 2097152 | tf_op jit(solution)/shard_map/psum | solution.py:111
  7.2 7.8 %collective-permute-start = (f32[2,2,256,384]{3,2,1,0:T(8,128)}, f32[2,2,256,384]{3,2,1,0:T(8,128)}, u32[]{:S(2)}, u32[]{:S(2)}) collective-permute-start(f32[2,2,256,384]{3,2,1,0:T(8,128)} %param.13), channel_id=1, source_target_pairs={{4,0},{8,4},{12,8},{16,12},{20,16},{24,20},{28,24},{5,1},{9,5},{13... | collective-permute-start | bytes 4718600 | tf_op jit(solution)/shard_map/ppermute | solution.py:17
  10.0 5.0 copy-start.17
  29.1 2.7 copy-start.10
  29.1 2.7 copy-start.12
  31.9 22.4 %copy-start.4 = (f32[4,256,256]{2,1,0:T(8,128)}, f32[4,256,256]{2,1,0:T(8,128)S(1)}, u32[]{:S(2)}) copy-start(f32[4,256,256]{2,1,0:T(8,128)S(1)} %get-tuple-element.90) | copy-start | bytes 3145732
  63.4 4.7 copy-start.8
  100.5 27.9 %copy-start = (f32[4,2,256,256]{3,2,1,0:T(8,128)}, f32[4,2,256,256]{3,2,1,0:T(8,128)S(1)}, u32[]{:S(2)}) copy-start(f32[4,2,256,256]{3,2,1,0:T(8,128)S(1)} %fusion.70) | copy-start | bytes 6291460
  104.9 23.5 %copy-start.2 = (f32[4,2,256,256]{3,2,1,0:T(8,128)}, f32[4,2,256,256]{3,2,1,0:T(8,128)S(1)}, u32[]{:S(2)}) copy-start(f32[4,2,256,256]{3,2,1,0:T(8,128)S(1)} %fusion.73) | copy-start | bytes 6291460
  137.7 7.2 %copy-start.6 = (f32[4,2,256,256]{3,2,1,0:T(8,128)}, f32[4,2,256,256]{3,2,1,0:T(8,128)S(1)}, u32[]{:S(2)}) copy-start(f32[4,2,256,256]{3,2,1,0:T(8,128)S(1)} %multiply_subtract_fusion.4) | copy-start | bytes 6291460
  144.9 386.1 %all-reduce.6.cloned.1.call-start = ((), (), s32[]{:S(2)}) async-start(), calls=%async_computation.1 | async-start | bytes 6291456 | tf_op jit(solution)/shard_map/psum | solution.py:125
  213.4 2.2 copy-start.14
  220.1 4.5 copy-start.7
  243.4 4.5 copy-start.1
  243.4 4.5 copy-start.3
  286.1 4.6 copy-start.9
  319.0 4.5 copy-start.5
  319.0 4.5 copy-start.11
  319.0 4.5 copy-start.13
  333.7 1.9 copy-start.18
  333.7 1.9 copy-start.19
  411.4 188.9 %all-reduce.8.cloned.1.call-start = ((), (), s32[]{:S(2)}) async-start(), calls=%async_computation.2 | async-start | bytes 2097152 | tf_op jit(solution)/shard_map/psum | solution.py:128
  531.0 5.5 copy-start.15
  533.9 68.7 %collective-permute-start.1 = (f32[2,2,256,384]{3,2,1,0:T(8,128)}, f32[2,2,256,384]{3,2,1,0:T(8,128)}, u32[]{:S(2)}, u32[]{:S(2)}) collective-permute-start(f32[2,2,256,384]{3,2,1,0:T(8,128)} %slice.80), channel_id=1, source_target_pairs={{0,4},{4,8},{8,12},{12,16},{16,20},{20,24},{24,28},{1,5},{5,9},{9,... | collective-permute-start | bytes 4718600 | tf_op jit(solution)/shard_map/ppermute | solution.py:17
  537.9 64.7 %copy-start.16 = (f32[2,2,512,384]{3,2,1,0:T(8,128)S(1)}, f32[2,2,512,384]{3,2,1,0:T(8,128)}, u32[]{:S(2)}) copy-start(f32[2,2,512,384]{3,2,1,0:T(8,128)} %all-reduce.6.cloned.1.call-done) | copy-start | bytes 9437188
Sparse Core Ops, SparseCore 0:
  145.0 68.3 all-reduce.3
  411.5 119.4 all-reduce.5
  538.0 62.2 all-reduce.7
where the time goes:
time: 624 us; the launch traced here: 612 us
  waiting for transfers between devices  250 us (40%)
  matrix products  228 us (37%)
  local copies, waits for them, and re-layouts  79.5 us (13%)
  other arithmetic  19.9 us (3%)
  loops' own time  15.6 us (2%)
  between operations  15.2 us (2%)
    psum x1, waiting for transfers between devices, per_device(): summed = lax.psum(grad_ext, 'mode')  120 us
    dot_general x24, matrix products, on_right(): return jnp.einsum('mjk,kl->mjl', field, matrix, precision=HIGH)  114 us
    dot_general x24, matrix products, on_left(): return jnp.einsum('jk,mkl->mjl', matrix, field, precision=HIGH)  114 us
    psum x1, waiting for transfers between devices, per_device(): power = lax.psum(local_power, 'mode')  67.6 us
    psum x1, waiting for transfers between devices, per_device(): probe_grad = lax.psum(grad_probe, 'tile')  62.4 us
    dynamic_update_slice x4, local copies, waits for them, and re-layouts, place_terms(): return lax.dynamic_update_slice(grad_ext, current + pieces, start)  47.2 us
    another operation x1, loops' own time, per_device(): lax.fori_loop(zero_index, jnp.full((), slot_total, jnp.int32), add_slot,...  15.6 us
    gather x12, local copies, waits for them, and re-layouts  12.5 us
  transfers between devices with their start and end apart: 5, of which 3 were waited for; matrix products, arithmetic and copies ran while one was open for 2% of the time, Pallas kernels for 0%

commit v1 on v0

v1 whole, which is shorter than its diff:
```python
import functools
import math

import jax
import jax.numpy as jnp
from jax import lax
from jax.experimental import pallas as pl
from jax.experimental.pallas import tpu as pltpu
from jax.sharding import PartitionSpec as P

F32 = jnp.float32
BF16 = jnp.bfloat16
VMEM_SPEC = pl.BlockSpec(memory_space=pltpu.VMEM)


def shifted(block, axis, distance):
    devices = range(lax.axis_size(axis))
    route = [(i - distance, i) for i in devices if i - distance in devices]
    return lax.ppermute(block, axis, route)


def dft_tables(length):
    indices = jnp.arange(length, dtype=jnp.int32)
    product = indices[:, None] * indices[None, :] % length
    angle = product.astype(F32) * (2.0 * math.pi / length)
    factor = 1.0 / math.sqrt(length)
    cosine, sine = jnp.cos(angle) * factor, jnp.sin(angle) * factor

    def parts(x):
        high = lax.reduce_precision(x, 8, 7)
        return high.astype(BF16), (x - high).astype(BF16)

    c_hi, c_lo = parts(cosine)
    s_hi, s_lo = parts(sine)
    plus_hi = jnp.block([[c_hi, -s_hi], [s_hi, c_hi]])
    plus_lo = jnp.block([[c_lo, -s_lo], [s_lo, c_lo]])
    minus_hi = jnp.block([[c_hi, s_hi], [-s_hi, c_hi]])
    minus_lo = jnp.block([[c_lo, s_lo], [-s_lo, c_lo]])
    left = jnp.stack([
        jnp.concatenate([minus_hi, minus_hi, minus_lo], axis=1),
        jnp.concatenate([plus_hi, plus_hi, plus_lo], axis=1),
    ])
    right = jnp.stack([
        jnp.concatenate([plus_hi, plus_hi, plus_lo], axis=0),
        jnp.concatenate([minus_hi, minus_hi, minus_lo], axis=0),
    ])
    return left, right


def split(x, axis):
    high = x.astype(BF16)
    low = (x - high.astype(F32)).astype(BF16)
    return jnp.concatenate([high, low, high], axis=axis)


def transform(real, imag, left_ref, right_ref, way):
    n = real.shape[0]
    stacked = split(jnp.concatenate([real, imag], axis=0), 0)
    mid = jnp.dot(left_ref[way], stacked, preferred_element_type=F32)
    wide = split(jnp.concatenate([mid[:n], mid[n:]], axis=1), 1)
    out = jnp.dot(wide, right_ref[way], preferred_element_type=F32)
    return out[:, :n], out[:, n:]


def times(a, b):
    return a[0] * b[0] - a[1] * b[1], a[0] * b[1] + a[1] * b[0]


def times_conj(a, b):
    return a[0] * b[0] + a[1] * b[1], a[0] * b[1] - a[1] * b[0]


def cut_windows(own_ref, next_ref, ext_ref, window_ref, row, col, first):
    layers, _, tile_rows, columns = own_ref.shape
    width = window_ref.shape[-1]

    @pl.when(first)
    def _():
        ext_ref[:, :, :tile_rows, :] = own_ref[...]
        ext_ref[:, :, tile_rows:, :] = next_ref[...]

    base = pl.multiple_of(row // 8 * 8, 8)
    extra = row - base
    turn = lax.rem(columns - col, columns)
    for layer in range(layers):
        for part in range(2):
            block = ext_ref[layer, part, pl.ds(base, width + 8), :]
            block = pltpu.roll(block, lax.rem(width + 8 - extra, width + 8), 0)[:width]
            window_ref[layer, part] = pltpu.roll(block, turn, 1)[:, :width]


def forward_kernel(count_ref, row_ref, col_ref, own_ref, next_ref, probe_ref, prop_ref, left_ref, right_ref,
                   before_ref, far_ref, power_ref, ext_ref, window_ref):
    slot, mode = pl.program_id(0), pl.program_id(1)
    alive = slot < count_ref[0]

    @pl.when(mode == 0)
    def _():
        cut_windows(own_ref, next_ref, ext_ref, window_ref, row_ref[slot], col_ref[slot], slot == 0)
        power_ref[...] = jnp.zeros_like(power_ref)

    @pl.when(alive)
    def _():
        wave = times((probe_ref[mode, 0], probe_ref[mode, 1]), (window_ref[0, 0], window_ref[0, 1]))
        spectrum = transform(*wave, left_ref, right_ref, 0)
        moved = transform(*times((prop_ref[0], prop_ref[1]), spectrum), left_ref, right_ref, 1)
        before_ref[0, 0, 0] = moved[0]
        before_ref[0, 0, 1] = moved[1]
        wave = times(moved, (window_ref[1, 0], window_ref[1, 1]))
        far = transform(*wave, left_ref, right_ref, 0)
        far_ref[0, 0, 0] = far[0]
        far_ref[0, 0, 1] = far[1]
        power_ref[0] += far[0] * far[0] + far[1] * far[1]


def backward_kernel(count_ref, row_ref, col_ref, own_ref, next_ref, probe_ref, prop_ref, left_ref, right_ref,
                    before_ref, far_ref, power_ref, measured_ref,
                    grad_ref, rim_ref, probe_grad_ref, ext_ref, window_ref, piece_ref, total_ref, *, modes):
    slot, mode = pl.program_id(0), pl.program_id(1)
    local_modes = pl.num_programs(1)
    alive = slot < count_ref[0]
    layers, _, tile_rows, columns = own_ref.shape
    width = window_ref.shape[-1]

    @pl.when((slot == 0) & (mode == 0))
    def _():
        total_ref[...] = jnp.zeros_like(total_ref)
        probe_grad_ref[...] = jnp.zeros_like(probe_grad_ref)

    @pl.when(mode == 0)
    def _():
        cut_windows(own_ref, next_ref, ext_ref, window_ref, row_ref[slot], col_ref[slot], slot == 0)
        piece_ref[...] = jnp.zeros_like(piece_ref)

    @pl.when(alive)
    def _():
        weight = (power_ref[0] - measured_ref[0]) / modes
        back = transform(weight * far_ref[0, 0, 0], weight * far_ref[0, 0, 1], left_ref, right_ref, 1)
        term = times_conj((before_ref[0, 0, 0], before_ref[0, 0, 1]), back)
        piece_ref[1, 0] += term[0]
        piece_ref[1, 1] += term[1]
        inner = transform(*times_conj((window_ref[1, 0], window_ref[1, 1]), back), left_ref, right_ref, 0)
        back = transform(*times_conj((prop_ref[0], prop_ref[1]), inner), left_ref, right_ref, 1)
        term = times_conj((probe_ref[mode, 0], probe_ref[mode, 1]), back)
        piece_ref[0, 0] += term[0]
        piece_ref[0, 1] += term[1]
        term = times_conj((window_ref[0, 0], window_ref[0, 1]), back)
        probe_grad_ref[mode, 0] += term[0]
        probe_grad_ref[mode, 1] += term[1]

    @pl.when(alive & (mode == local_modes - 1))
    def _():
        row, col = row_ref[slot], col_ref[slot]
        base = pl.multiple_of(row // 8 * 8, 8)
        extra = row - base
        for layer in range(layers):
            for part in range(2):
                block = piece_ref[layer, part]
                block = jnp.concatenate([block, jnp.zeros((width, columns - width), F32)], axis=1)
                block = pltpu.roll(block, col, 1)
                block = jnp.concatenate([block, jnp.zeros((8, columns), F32)], axis=0)
                block = pltpu.roll(block, extra, 0)
                total_ref[layer, part, pl.ds(base, width + 8), :] += block

    @pl.when((slot == pl.num_programs(0) - 1) & (mode == local_modes - 1))
    def _():
        grad_ref[...] = total_ref[:, :, :tile_rows, :]
        rim_ref[...] = total_ref[:, :, tile_rows:, :]


def per_device(object_field, probe, measured, prop_phase, counts, row_offset, col_offset):
    layers, _, tile_rows, columns = object_field.shape
    width = probe.shape[-1]
    local_modes = probe.shape[0]
    modes = local_modes * lax.axis_size("mode")
    slots = row_offset.shape[0]
    next_rows = shifted(object_field, "tile", -1)
    left, right = dft_tables(width)
    prop = jnp.stack([jnp.cos(prop_phase), jnp.sin(prop_phase)])

    per_mode = pl.BlockSpec((1, 1, 2, width, width), lambda s, m, *_: (s, m, 0, 0, 0))
    per_slot = pl.BlockSpec((1, width, width), lambda s, m, *_: (s, 0, 0))
    ext_shape = pltpu.VMEM((layers, 2, tile_rows + width, columns), F32)
    window_shape = pltpu.VMEM((layers, 2, width, width), F32)
    field = jax.ShapeDtypeStruct((slots, local_modes, 2, width, width), F32)
    params = pltpu.CompilerParams(dimension_semantics=("arbitrary", "arbitrary"), vmem_limit_bytes=60 << 20)

    before, far, local_power = pl.pallas_call(
        forward_kernel,
        out_shape=(field, field, jax.ShapeDtypeStruct((slots, width, width), F32)),
        grid_spec=pltpu.PrefetchScalarGridSpec(
            num_scalar_prefetch=3,
            grid=(slots, local_modes),
            in_specs=[VMEM_SPEC] * 6,
            out_specs=(per_mode, per_mode, per_slot),
            scratch_shapes=[ext_shape, window_shape],
        ),
        compiler_params=params,
        name="forward",
    )(counts, row_offset, col_offset, object_field, next_rows, probe, prop, left, right)

    power = lax.psum(local_power, "mode")

    whole = lambda shape: pl.BlockSpec(shape, lambda s, m, *_: (0,) * len(shape))
    grad, rim, grad_probe = pl.pallas_call(
        functools.partial(backward_kernel, modes=modes),
        out_shape=(
            jax.ShapeDtypeStruct(object_field.shape, F32),
            jax.ShapeDtypeStruct((layers, 2, width, columns), F32),
            jax.ShapeDtypeStruct(probe.shape, F32),
        ),
        grid_spec=pltpu.PrefetchScalarGridSpec(
            num_scalar_prefetch=3,
            grid=(slots, local_modes),
            in_specs=[VMEM_SPEC] * 6 + [per_mode, per_mode, per_slot, per_slot],
            out_specs=(whole(object_field.shape), whole((layers, 2, width, columns)), whole(probe.shape)),
            scratch_shapes=[ext_shape, window_shape, window_shape, ext_shape],
        ),
        compiler_params=params,
        name="backward",
    )(counts, row_offset, col_offset, object_field, next_rows, probe, prop, left, right, before, far, power, measured)

    arrived = shifted(rim, "tile", 1)
    object_grad = lax.psum(grad.at[:, :, :width, :].add(arrived), "mode")
    probe_grad = lax.psum(grad_probe, "tile")
    return (object_grad, probe_grad)


def solution(mesh):
    placed = (
        P(None, None, "tile", None),
        P("mode", None, None, None),
        P("tile", None, None),
        P(),
        P("tile"),
        P("tile"),
        P("tile"),
    )
    return jax.shard_map(
        per_device,
        mesh=mesh,
        in_specs=placed,
        out_specs=(P(None, None, "tile", None), P("mode", None, None, None)),
        check_vma=False,
    )
```

time: 624 us -> 351 us (0.56); the launches traced: 612 us -> 351 us
  matrix products: 228 us -> 0 us
  local copies, waits for them, and re-layouts: 79.5 us -> 6.53 us
  Pallas kernels: 0 us -> 68.2 us
  waiting for transfers between devices: 250 us -> 222 us
  other arithmetic: 19.9 us -> 36.9 us
  loops' own time: 15.6 us -> 0 us
    dot_general x48 -> x0, matrix products: 228 us -> none  [the longest x24 114 us: on_right(): return jnp.einsum('mjk,kl->mjl', field, matrix, precision=HIGH)]
    pallas_call x0 -> x2, Pallas kernels: none -> 68.2 us  [the longest x1 36.8 us: per_device(): pl.pallas_call(functools.partial(backward_kernel, modes=modes), out_shape...]
    psum x1, waiting for transfers between devices: 120 us -> 71.2 us  [per_device(): object_grad = lax.psum(grad.at[:, :, :width, :].add(arrived), 'mode')]
    dynamic_update_slice x4 -> x0, local copies, waits for them, and re-layouts: 47.2 us -> none  [place_terms(): return lax.dynamic_update_slice(grad_ext, current + pieces, start)]
    another operation x1 -> x5, other arithmetic: 0.27 us -> 30.7 us  [the longest x3 27.8 us: dft_tables(): jnp.stack([jnp.concatenate([minus_hi, minus_hi, minus_lo], axis=1), jnp.c...]
    another operation x2 -> x0, loops' own time: 15.6 us -> none  [the longest x1 15.6 us: per_device(): lax.fori_loop(zero_index, jnp.full((), slot_total, jnp.int32), add_slot,...]
    gather x12 -> x0, local copies, waits for them, and re-layouts: 12.5 us -> none
    psum x1, waiting for transfers between devices: 62.4 us -> 73.1 us  [per_device(): probe_grad = lax.psum(grad_probe, 'tile')]
  transfers between devices with their start and end apart: 5 -> 5, of which waited for: 3 -> 4; matrix products, arithmetic and copies ran while one was open for 2% -> 11% of each run, Pallas kernels for 0% -> 0%
where the time goes in v1:
time: 351 us
  waiting for transfers between devices  222 us (63%)
  Pallas kernels  68.2 us (19%)
  other arithmetic  36.9 us (11%)
  between operations  14.5 us (4%)
  local copies, waits for them, and re-layouts  6.53 us (2%)
    psum x1, waiting for transfers between devices, per_device(): power = lax.psum(local_power, 'mode')  74.2 us
    psum x1, waiting for transfers between devices, per_device(): probe_grad = lax.psum(grad_probe, 'tile')  73.1 us
    psum x1, waiting for transfers between devices, per_device(): object_grad = lax.psum(grad.at[:, :, :width, :].add(arrived), 'mode')  71.2 us
    pallas_call x1, Pallas kernels, per_device(): pl.pallas_call(functools.partial(backward_kernel, modes=modes), out_shape...  36.8 us
    pallas_call x1, Pallas kernels, per_device(): pl.pallas_call(forward_kernel, out_shape=(field, field, jax.ShapeDtypeStr...  31.4 us
    another operation x3, other arithmetic, dft_tables(): jnp.stack([jnp.concatenate([minus_hi, minus_hi, minus_lo], axis=1), jnp.c...  27.8 us
  transfers between devices with their start and end apart: 5, of which 4 were waited for; matrix products, arithmetic and copies ran while one was open for 11% of the time, Pallas kernels for 0%

profile of v1, /device:TPU:0, one launch (start us, length us, event | category | flops | bytes accessed | tf_op | source)
XLA Modules:
  0.0 350.6 jit_solution(3986122910193736505)
XLA Ops:
  7.2 0.0 all-reduce.4.cloned.1.call-start
  7.2 1.3 collective-permute-start
  8.5 1.0 fusion.32
  9.5 1.1 fusion.16
  10.7 1.1 reduce-precision_convert_fusion
  12.6 13.2 %fusion.7 = bf16[1,512,1536]{2,1,0:T(8,128)(2,1)S(1)} fusion(bf16[256,256]{1,0:T(8,128)(2,1)S(1)} %get-tuple-element.45, bf16[256,256]{1,0:T(8,128)(2,1)S(1)} %get-tuple-element.46, bf16[256,256]{1,0:T(8,128)(2,1)S(1)} %get-tuple-element.47, bf16[256,256]{1,0:T(8,128)(2,1)S(1)} %get-tuple-element.48, bf16[256,256]{1,0:T(8,128)(2,1)S(1)} %get-tuple-element.44, ...), kind=kLoop, calls=%fused_computation.21 | loop fusion | flops 18874368 | bytes 2359296 | tf_op jit(solution)/shard_map/stack | solution.py:39
  25.9 0.0 copy-start.2
  26.0 0.8 copy-done.2
  26.8 0.9 cosine_bitcast_fusion
  27.8 0.8 pad_maximum_fusion.14.prop_ref
  28.6 12.6 %fusion.3 = bf16[1,512,1536]{2,1,0:T(8,128)(2,1)S(1)} fusion(bf16[256,256]{1,0:T(8,128)(2,1)S(1)} %get-tuple-element.45, bf16[256,256]{1,0:T(8,128)(2,1)S(1)} %get-tuple-element.46, bf16[256,256]{1,0:T(8,128)(2,1)S(1)} %get-tuple-element.48, bf16[256,256]{1,0:T(8,128)(2,1)S(1)} %get-tuple-element.47, bf16[256,256]{1,0:T(8,128)(2,1)S(1)} %get-tuple-element.49, ...), kind=kLoop, calls=%fused_computation.17 | loop fusion | flops 18874368 | bytes 2359296 | tf_op jit(solution)/shard_map/stack | solution.py:39
  41.2 2.0 pad_maximum_fusion.left_ref
  43.2 2.0 pad_maximum_fusion.1.right_ref
  45.2 0.0 collective-permute-done.next_ref
  45.2 0.0 copy-start
  45.2 1.1 copy-done
  46.3 31.4 %forward.1 = (f32[4,2,2,256,256]{4,3,2,1,0:T(8,128)}, f32[4,2,2,256,256]{4,3,2,1,0:T(8,128)}, f32[4,256,256]{2,1,0:T(8,128)}) custom-call(s32[1]{0:T(128)S(6)} %copy.22.count_ref, s32[4]{0:T(128)} %row_ref.3, s32[4]{0:T(128)} %col_ref.3, f32[2,2,256,384]{3,2,1,0:T(8,128)} %own_ref.3, f32[2,2,256,384]{3,2,1,0:T(8,128)} %copy-done, ...), custom_call_target="tpu_custom_call" | custom-call | tf_op jit(solution)/shard_map/forward/pallas_call | solution.py:188
  77.8 0.0 all-reduce.4.cloned.1.call-update
  77.8 0.0 all-reduce.8.cloned.1.call-start
  77.9 74.2 %all-reduce.4.cloned.1.call-done.power_ref = f32[4,256,256]{2,1,0:T(8,128)} async-done(((f32[4,256,256]{2,1,0:T(8,128)}), f32[4,256,256]{2,1,0:T(8,128)}) %all-reduce.4.cloned.1.call-update) | async-done | bytes 1048592 | tf_op jit(solution)/shard_map/psum | solution.py:202
  152.1 36.8 %backward.1 = (f32[2,2,256,384]{3,2,1,0:T(8,128)}, f32[2,2,256,384]{3,2,1,0:T(8,128)}, f32[2,2,256,256]{3,2,1,0:T(8,128)}) custom-call(s32[1]{0:T(128)S(6)} %copy.22.count_ref, s32[4]{0:T(128)} %row_ref.3, s32[4]{0:T(128)} %col_ref.3, f32[2,2,256,384]{3,2,1,0:T(8,128)} %own_ref.3, f32[2,2,256,384]{3,2,1,0:T(8,128)} %copy-done, f32[2,2,256,256]{3,2,1,0:T(8,128)} %probe_ref.3, ...), custom_call_target="tpu_custom_call" | custom-call | tf_op jit(solution)/shard_map/backward/pallas_call | solution.py:205
  188.9 1.4 collective-permute-start.1
  190.2 0.0 all-reduce.8.cloned.1.call-update
  190.3 0.0 all-reduce.6.cloned.1.call-start
  190.3 3.1 collective-permute-done.1
  193.4 2.7 add.52
  196.1 0.0 all-reduce.6.cloned.1.call-update
  196.1 73.1 %all-reduce.8.cloned.1.call-done = f32[2,2,256,256]{3,2,1,0:T(8,128)} async-done(((f32[2,2,256,256]{3,2,1,0:T(8,128)}), f32[2,2,256,256]{3,2,1,0:T(8,128)}) %all-reduce.8.cloned.1.call-update) | async-done | bytes 1048592 | tf_op jit(solution)/shard_map/psum | solution.py:225
  269.3 71.2 %all-reduce.6.cloned.1.call-done = f32[2,2,256,384]{3,2,1,0:T(8,128)} async-done(((f32[2,2,256,384]{3,2,1,0:T(8,128)}), f32[2,2,256,384]{3,2,1,0:T(8,128)}) %all-reduce.6.cloned.1.call-update) | async-done | bytes 1572880 | tf_op jit(solution)/shard_map/psum | solution.py:224
  340.4 2.7 copy.23
  343.1 0.0 copy-done.1
  343.1 1.0 copy.24
  (9 shorter events, 0.2 us)
Async XLA Ops:
  7.2 144.9 %all-reduce.4.cloned.1.call-start = ((), (), s32[]{:S(2)}) async-start(), calls=%async_computation | async-start | bytes 2097152 | tf_op jit(solution)/shard_map/psum | solution.py:202
  7.2 38.0 %collective-permute-start = (f32[2,2,256,384]{3,2,1,0:T(8,128)}, f32[2,2,256,384]{3,2,1,0:T(8,128)S(1)}, u32[]{:S(2)}, u32[]{:S(2)}) collective-permute-start(f32[2,2,256,384]{3,2,1,0:T(8,128)} %own_ref.3), channel_id=1, source_target_pairs={{4,0},{8,4},{12,8},{16,12},{20,16},{24,20},{28,24},{5,1},{9,5},{13... | collective-permute-start | bytes 4718600 | tf_op jit(solution)/shard_map/ppermute | solution.py:19
  25.9 1.0 copy-start.2
  45.2 1.1 copy-start
  77.8 191.5 %all-reduce.8.cloned.1.call-start = ((), (), s32[]{:S(2)}) async-start(), calls=%async_computation.2 | async-start | bytes 2097152 | tf_op jit(solution)/shard_map/psum | solution.py:225
  188.9 4.5 %collective-permute-start.1 = (f32[2,2,256,384]{3,2,1,0:T(8,128)}, f32[2,2,256,384]{3,2,1,0:T(8,128)S(1)}, u32[]{:S(2)}, u32[]{:S(2)}) collective-permute-start(f32[2,2,256,384]{3,2,1,0:T(8,128)} %get-tuple-element.32), channel_id=1, source_target_pairs={{0,4},{4,8},{8,12},{12,16},{16,20},{20,24},{24,28},{1,5},{5,9},{9,... | collective-permute-start | bytes 4718600 | tf_op jit(solution)/shard_map/ppermute | solution.py:19
  190.3 150.2 %all-reduce.6.cloned.1.call-start = ((), (), s32[]{:S(2)}) async-start(), calls=%async_computation.1 | async-start | bytes 3145728 | tf_op jit(solution)/shard_map/psum | solution.py:224
  269.3 73.8 %copy-start.1 = (f32[2,2,256,256]{3,2,1,0:T(8,128)S(1)}, f32[2,2,256,256]{3,2,1,0:T(8,128)}, u32[]{:S(2)}) copy-start(f32[2,2,256,256]{3,2,1,0:T(8,128)} %all-reduce.8.cloned.1.call-done) | copy-start | bytes 3145732
Sparse Core Ops, SparseCore 0:
  77.9 74.1 all-reduce.3
  190.4 78.8 all-reduce.7
  272.2 68.1 all-reduce.5
